TPU v7x, 32 devices: a whole 2x2x4 slice. The times are simulated.
32 devices in a mesh: blk: 8 (over y, x, core), slab: 4 (over z).
Axes of the slice: x: 2, y: 2, z: 4, core: 2. Of those that a mesh axis runs over, the one named last changes fastest.
Arguments:
- old_factor: bfloat16 [8192, 24576], P('slab', 'blk'), may hold values from -0.0546875 to 0.0546875
- solved: bfloat16 [24576, 256], P('blk', 'slab'), may hold values from -6 to 6
- band: bfloat16 [8192, 8192], P('blk'), may hold values from -0.0625 to 0.0625
- inv_diag: bfloat16 [2048, 8192], P(None, 'blk'), may hold values from -1 to 2, as said below
- rhs: bfloat16 [8192, 256], P('blk', 'slab'), may hold values from -6 to 6
Outputs:
- solution: bfloat16 [8192, 256], P('blk', 'slab')
Inputs may be any that keep to these rules, and one draw needn't show every extreme that they name: `inv_diag`: columns k * 2048 to (k + 1) * 2048 - 1 hold the inverse applied in block step k.
All inputs are finite; a program needn't handle non-finite values.
Results may differ from a plain program's by a relative error of at most 0.008.
Values may be sent and summed in bfloat16 or wider, within the bound.
A program may use at most 64 MiB of HBM per device.

v0:
```python
import jax
import jax.numpy as jnp
from jax import lax
from jax.sharding import PartitionSpec as P

STEPS = 4


def body(old_factor, solved, band, inv_diag, rhs):
    own_rows = rhs.shape[0]
    block_rows = inv_diag.shape[0]
    group_size = block_rows // own_rows
    own_index = lax.axis_index("blk")
    own_block = own_index // group_size
    offset = own_index % group_size * own_rows
    partial_value = jnp.dot(
        old_factor,
        lax.all_gather(solved, "slab", axis=1, tiled=True),
        preferred_element_type=jnp.float32,
    )
    window_terms = lax.all_to_all(partial_value, "slab", split_axis=1, concat_axis=0, tiled=True)
    source = rhs.astype(jnp.float32)
    accum = lax.psum_scatter(window_terms, "blk", scatter_dimension=0, tiled=True)
    solution = jnp.zeros(rhs.shape, jnp.bfloat16)
    for step in range(STEPS):
        total = accum
        resid = (source - total).astype(jnp.bfloat16)
        term = jnp.dot(inv_diag, resid, preferred_element_type=jnp.float32)
        term = jnp.where(own_block == step, term, jnp.zeros_like(term))
        newest = lax.psum(term, "blk").astype(jnp.bfloat16)
        mine = lax.dynamic_slice_in_dim(newest, offset, own_rows, 0)
        solution = jnp.where(own_block == step, mine, solution)
        if step + 1 < STEPS:
            columns = band[:, step * block_rows : (step + 1) * block_rows]
            update = jnp.dot(columns, newest, preferred_element_type=jnp.float32)
            accum = accum + jnp.where(own_block > step, update, jnp.zeros_like(update))
    return solution


def solution(mesh):
    return jax.shard_map(
        body,
        mesh=mesh,
        in_specs=(
            P("slab", "blk"),
            P("blk", "slab"),
            P("blk", None),
            P(None, "blk"),
            P("blk", "slab"),
        ),
        out_specs=P("blk", "slab"),
        check_vma=False,
    )
```

profile of v0, /device:TPU:0, one launch (start us, length us, event | category | flops | bytes accessed | tf_op | source)
XLA Modules:
  0.0 292.5 jit_solution(17000383142873836997)
XLA Ops:
  6.5 0.0 all-gather.2.cloned.1.call-start
  6.5 0.7 all-gather.2.cloned.1.call-update
  7.3 0.0 reduce-scatter.2.cloned.1.call-start
  7.3 41.4 %all-gather.2.cloned.1.call-done = bf16[3072,256]{0,1:T(8,128)(2,1)} async-done(((bf16[3072,64]{0,1:T(8,128)(2,1)}), bf16[3072,256]{0,1:T(8,128)(2,1)}) %all-gather.2.cloned.1.call-update) | async-done | bytes 1572880 | tf_op jit(solution)/shard_map/all_gather | solution.py:18
  48.7 6.9 %fusion.56 = f32[2048,256]{0,1:T(8,128)S(1)} fusion(bf16[2048,3072]{1,0:T(8,128)(2,1)} %param.5, bf16[3072,256]{0,1:T(8,128)(2,1)} %all-gather.2.cloned.1.call-done), kind=kOutput, calls=%fused_computation.37 | convolution fusion | flops 3221225472 | bytes 16252928 | tf_op jit(solution)/shard_map/dot_general | solution.py:16
  55.6 50.4 %all_to_all.19 = f32[2048,4,64]{0,2,1:T(8,128)S(1)} all-to-all(f32[2048,4,64]{0,2,1:T(8,128)S(1)} %bitcast.41), channel_id=1, replica_groups=mesh['blk'=8,'slab'=4] {'slab'}, dimensions={1} | all-to-all | bytes 4194304 | tf_op jit(solution)/shard_map/all_to_all | solution.py:21
  106.0 0.0 copy-start.2
  106.0 1.5 copy.7
  107.5 0.0 reduce-scatter.2.cloned.1.call-update
  107.6 40.6 %reduce-scatter.2.cloned.1.call-done = f32[1024,64]{0,1:T(8,128)} async-done(((f32[8192,64]{0,1:T(8,128)}), f32[1024,64]{0,1:T(8,128)}) %reduce-scatter.2.cloned.1.call-update) | async-done | bytes 262160 | tf_op jit(solution)/shard_map/reduce_scatter | solution.py:23
  148.2 0.0 copy-done.2
  148.2 0.0 copy-start.3
  148.2 3.7 %fusion.6 = f32[2048,64]{0,1:T(8,128)S(1)} fusion(bf16[2048,1024]{1,0:T(8,128)(2,1)} %param.8, pred[]{:T(512)S(6)} %eq.19, f32[1024,64]{0,1:T(8,128)} %reduce-scatter.2.cloned.1.call-done, bf16[1024,64]{0,1:T(8,128)(2,1)S(1)} %copy-done.2), kind=kOutput, calls=%fused_computation.10 | convolution fusion | flops 268763136 | bytes 5111809 | tf_op jit(solution)/shard_map/dot_general | solution.py:28
  151.9 29.6 %all-reduce.4 = bf16[2048,64]{0,1:T(8,128)(2,1)S(1)} all-reduce(f32[2048,64]{0,1:T(8,128)S(1)} %fusion.6), channel_id=1, replica_groups=mesh['blk'=8,'slab'=4] {'blk'}, use_global_device_ids=true, to_apply=%region_1.2 | all-reduce | flops 131072 | bytes 786432 | tf_op jit(solution)/shard_map/psum | solution.py:30
  181.5 0.0 copy-done.3
  181.5 0.0 copy-start
  181.5 3.7 %fusion.16 = f32[1024,64]{0,1:T(8,128)S(1)} fusion(f32[1024,64]{0,1:T(8,128)S(1)} %copy-done.3, bf16[2048,64]{0,1:T(8,128)(2,1)S(1)} %all-reduce.4, bf16[1024,8192]{1,0:T(8,128)(2,1)} %param.7, pred[]{:T(512)S(6)} %gt.9), kind=kOutput, calls=%fused_computation.16 | convolution fusion | flops 268566528 | bytes 4980737 | tf_op jit(solution)/shard_map/dot_general | solution.py:35
  185.3 0.0 copy-done
  185.3 1.4 fusion.7
  186.7 29.4 %all-reduce.5 = bf16[2048,64]{0,1:T(8,128)(2,1)S(1)} all-reduce(f32[2048,64]{0,1:T(8,128)S(1)} %fusion.7), channel_id=1, replica_groups=mesh['blk'=8,'slab'=4] {'blk'}, use_global_device_ids=true, to_apply=%region_2.3 | all-reduce | flops 131072 | bytes 786432 | tf_op jit(solution)/shard_map/psum | solution.py:30
  216.1 0.0 copy-start.1
  216.1 3.7 %fusion.25 = f32[1024,64]{0,1:T(8,128)S(1)} fusion(f32[1024,64]{0,1:T(8,128)S(1)} %fusion.16, bf16[2048,64]{0,1:T(8,128)(2,1)S(1)} %all-reduce.5, bf16[1024,8192]{1,0:T(8,128)(2,1)} %param.7, pred[]{:T(512)S(6)} %gt.10), kind=kOutput, calls=%fused_computation.19 | convolution fusion | flops 268566528 | bytes 4980737 | tf_op jit(solution)/shard_map/dot_general | solution.py:35
  219.8 0.0 copy-done.1
  219.8 1.4 fusion.8
  221.2 28.8 %all-reduce.6 = bf16[2048,64]{0,1:T(8,128)(2,1)S(1)} all-reduce(f32[2048,64]{0,1:T(8,128)S(1)} %fusion.8), channel_id=1, replica_groups=mesh['blk'=8,'slab'=4] {'blk'}, use_global_device_ids=true, to_apply=%region_3.4 | all-reduce | flops 131072 | bytes 786432 | tf_op jit(solution)/shard_map/psum | solution.py:30
  250.0 6.2 %fusion.9 = f32[2048,64]{0,1:T(8,128)S(1)} fusion(bf16[2048,1024]{1,0:T(8,128)(2,1)} %param.8, f32[1024,64]{0,1:T(8,128)S(1)} %fusion.25, bf16[2048,64]{0,1:T(8,128)(2,1)S(1)} %all-reduce.6, bf16[1024,8192]{1,0:T(8,128)(2,1)} %param.7, bf16[1024,64]{0,1:T(8,128)(2,1)S(1)} %copy-done.2, pred[]{:T(512)S(6)} %eq.18, pred[]{:T(512)S(6)} %gt.11), kind=kOutput, calls=%fused_computation.13 | convolution fusion | flops 537329664 | bytes 9568258 | tf_op jit(solution)/shard_map/dot_general | solution.py:28
  256.2 28.8 %all-reduce.7 = bf16[2048,64]{0,1:T(8,128)(2,1)S(1)} all-reduce(f32[2048,64]{0,1:T(8,128)S(1)} %fusion.9), channel_id=1, replica_groups=mesh['blk'=8,'slab'=4] {'blk'}, use_global_device_ids=true, to_apply=%region_4.5 | all-reduce | flops 131072 | bytes 786432 | tf_op jit(solution)/shard_map/psum | solution.py:30
  284.9 0.7 fusion.49
Async XLA Ops:
  6.5 42.1 %all-gather.2.cloned.1.call-start = ((), (), s32[]{:S(2)}) async-start(), calls=%async_computation.2 | async-start | bytes 1966080 | tf_op jit(solution)/shard_map/all_gather | solution.py:18
  7.3 140.9 %reduce-scatter.2.cloned.1.call-start = ((), (), s32[]{:S(2)}) async-start(), calls=%async_computation.3 | async-start | bytes 2359296 | tf_op jit(solution)/shard_map/reduce_scatter | solution.py:23
  106.0 42.2 %copy-start.2 = (bf16[1024,64]{0,1:T(8,128)(2,1)S(1)}, bf16[1024,64]{0,1:T(8,128)(2,1)}, u32[]{:S(2)}) copy-start(bf16[1024,64]{0,1:T(8,128)(2,1)} %param.9) | copy-start | bytes 393220
  148.2 33.3 %copy-start.3 = (f32[1024,64]{0,1:T(8,128)S(1)}, f32[1024,64]{0,1:T(8,128)}, u32[]{:S(2)}) copy-start(f32[1024,64]{0,1:T(8,128)} %reduce-scatter.2.cloned.1.call-done) | copy-start | bytes 786436
  181.5 3.7 %copy-start = (bf16[2048,1024]{1,0:T(8,128)(2,1)S(1)}, bf16[2048,1024]{1,0:T(8,128)(2,1)}, u32[]{:S(2)}) copy-start(bf16[2048,1024]{1,0:T(8,128)(2,1)} %param.8) | copy-start | bytes 12582916
  216.1 3.7 %copy-start.1 = (bf16[2048,1024]{1,0:T(8,128)(2,1)S(1)}, bf16[2048,1024]{1,0:T(8,128)(2,1)}, u32[]{:S(2)}) copy-start(bf16[2048,1024]{1,0:T(8,128)(2,1)} %param.8) | copy-start | bytes 12582916
Sparse Core Ops, SparseCore 0:
  8.9 39.7 all-gather.1
  107.7 40.4 reduce-scatter.1
where the time goes:
time: 293 us
  blocking collectives  167 us (57%)
  waiting for transfers between devices  82.7 us (28%)
  matrix products  27 us (9%)
  between operations  13.5 us (5%)
    psum x4, blocking collectives, body(): newest = lax.psum(term, 'blk').astype(jnp.bfloat16)  117 us
    all_to_all x1, blocking collectives, body(): lax.all_to_all(partial_value, 'slab', split_axis=1, concat_axis=0, tiled=...  50.4 us
    all_gather x1, waiting for transfers between devices, body(): lax.all_gather(solved, 'slab', axis=1, tiled=True)  41.4 us
    reduce_scatter x1, waiting for transfers between devices, body(): lax.psum_scatter(window_terms, 'blk', scatter_dimension=0, tiled=True)  40.6 us
    dot_general x4, matrix products, body(): term = jnp.dot(inv_diag, resid, preferred_element_type=jnp.float32)  12.6 us
    dot_general x2, matrix products, body(): update = jnp.dot(columns, newest, preferred_element_type=jnp.float32)  7.47 us
    dot_general x1, matrix products, body(): jnp.dot(old_factor, lax.all_gather(solved, 'slab', axis=1, tiled=True), p...  6.89 us
  transfers between devices with their start and end apart: 2, of which 2 were waited for; matrix products, arithmetic and copies ran while one was open for 0% of the time, Pallas kernels for 0%

commit v1 on v0

--- a/solution.py
+++ b/solution.py
@@ -4,6 +4,18 @@
 from jax.sharding import PartitionSpec as P
 
 STEPS = 4
+
+
+def collect(array, axis, dim):
+    ways, here = (lax.axis_size(axis), lax.axis_index(axis))
+    grown, reach = (array, 1)
+    while reach < ways:
+        theirs = lax.ppermute(grown, axis, [(d, d ^ reach) for d in range(ways)])
+        mine_first = jnp.concatenate([grown, theirs], axis=dim)
+        theirs_first = jnp.concatenate([theirs, grown], axis=dim)
+        grown = jnp.where(here & reach == 0, mine_first, theirs_first)
+        reach = 2 * reach
+    return grown
 
 
 def body(old_factor, solved, band, inv_diag, rhs):
@@ -14,9 +26,7 @@
     own_block = own_index // group_size
     offset = own_index % group_size * own_rows
     partial_value = jnp.dot(
-        old_factor,
-        lax.all_gather(solved, "slab", axis=1, tiled=True),
-        preferred_element_type=jnp.float32,
+        old_factor, collect(solved, "slab", 1), preferred_element_type=jnp.float32
     )
     window_terms = lax.all_to_all(partial_value, "slab", split_axis=1, concat_axis=0, tiled=True)
     source = rhs.astype(jnp.float32)

time: 293 us -> 302 us (1.031)
  starting transfers between devices: 0.04 us -> 5.88 us
    ppermute x0 -> x2, waiting for transfers between devices: none -> 43 us  [collect(): theirs = lax.ppermute(grown, axis, [(d, d ^ reach) for d in range(ways)])]
    all_gather x1 -> x0, waiting for transfers between devices: 41.4 us -> none  [body(): lax.all_gather(solved, 'slab', axis=1, tiled=True)]
    ppermute x0 -> x2, starting transfers between devices: none -> 5.87 us  [collect(): theirs = lax.ppermute(grown, axis, [(d, d ^ reach) for d in range(ways)])]
  transfers between devices with their start and end apart: 2 -> 3, of which waited for: 2 -> 3; matrix products, arithmetic and copies ran while one was open for 0% -> 0% of each run, Pallas kernels for 0% -> 0%
where the time goes in v1:
time: 302 us
  blocking collectives  169 us (56%)
  waiting for transfers between devices  83.4 us (28%)
  matrix products  26.6 us (9%)
  between operations  13.5 us (4%)
  starting transfers between devices  5.88 us (2%)
    psum x4, blocking collectives, body(): newest = lax.psum(term, 'blk').astype(jnp.bfloat16)  116 us
    all_to_all x1, blocking collectives, body(): lax.all_to_all(partial_value, 'slab', split_axis=1, concat_axis=0, tiled=...  52.8 us
    ppermute x2, waiting for transfers between devices, collect(): theirs = lax.ppermute(grown, axis, [(d, d ^ reach) for d in range(ways)])  43 us
    reduce_scatter x1, waiting for transfers between devices, body(): lax.psum_scatter(window_terms, 'blk', scatter_dimension=0, tiled=True)  40.3 us
    dot_general x4, matrix products, body(): term = jnp.dot(inv_diag, resid, preferred_element_type=jnp.float32)  12.6 us
    dot_general x2, matrix products, body(): update = jnp.dot(columns, newest, preferred_element_type=jnp.float32)  7.47 us
    dot_general x1, matrix products, body(): jnp.dot(old_factor, collect(solved, 'slab', 1), preferred_element_type=jn...  6.46 us
  transfers between devices with their start and end apart: 3, of which 3 were waited for; matrix products, arithmetic and copies ran while one was open for 0% of the time, Pallas kernels for 0%

profile of v1, /device:TPU:0, one launch (start us, length us, event | category | flops | bytes accessed | tf_op | source)
XLA Modules:
  0.0 302.1 jit_solution(4494129183030168565)
XLA Ops:
  6.5 0.0 reduce-scatter.2.cloned.1.call-start
  6.5 3.1 %collective-permute-start = (bf16[3072,64]{0,1:T(8,128)(2,1)}, bf16[3072,64]{0,1:T(8,128)(2,1)S(1)}, u32[]{:S(2)}, u32[]{:S(2)}) collective-permute-start(bf16[3072,64]{0,1:T(8,128)(2,1)} %param.6), channel_id=1, source_target_pairs={{0,1},{1,0},{2,3},{3,2},{4,5},{5,4},{6,7},{7,6},{8,9},{9,8},{10,11... | collective-permute-start | bytes 1179656 | tf_op jit(solution)/shard_map/ppermute | solution.py:13
  9.6 9.3 %collective-permute-done = bf16[3072,64]{0,1:T(8,128)(2,1)S(1)} collective-permute-done((bf16[3072,64]{0,1:T(8,128)(2,1)}, bf16[3072,64]{0,1:T(8,128)(2,1)S(1)}, u32[]{:S(2)}, u32[]{:S(2)}) %collective-permute-start) | collective-permute-done | bytes 393248 | tf_op jit(solution)/shard_map/ppermute | solution.py:13
  18.9 1.3 maximum_select_fusion.2
  20.3 2.8 collective-permute-start.1
  23.1 33.7 %collective-permute-done.1 = bf16[3072,128]{0,1:T(8,128)(2,1)S(1)} collective-permute-done((bf16[3072,128]{0,1:T(8,128)(2,1)S(1)}, bf16[3072,128]{0,1:T(8,128)(2,1)S(1)}, u32[]{:S(2)}, u32[]{:S(2)}) %collective-permute-start.1) | collective-permute-done | bytes 786464 | tf_op jit(solution)/shard_map/ppermute | solution.py:13
  56.8 6.5 %fusion.10 = f32[256,2048]{1,0:T(8,128)S(1)} fusion(bf16[2048,3072]{1,0:T(8,128)(2,1)} %param.5, bf16[3072,128]{0,1:T(8,128)(2,1)S(1)} %collective-permute-done.1, bf16[3072,128]{0,1:T(8,128)(2,1)S(1)} %maximum_select_fusion.2, pred[]{:T(512)S(6)} %eq.25), kind=kOutput, calls=%fused_computation.15 | convolution fusion | flops 3228303360 | bytes 16252929 | tf_op jit(solution)/shard_map/dot_general | solution.py:28
  63.2 52.8 %all_to_all.19 = f32[2048,4,64]{0,2,1:T(8,128)S(1)} all-to-all(f32[2048,4,64]{0,2,1:T(8,128)S(1)} %bitcast.42), channel_id=1, replica_groups=mesh['blk'=8,'slab'=4] {'slab'}, dimensions={1} | all-to-all | bytes 4194304 | tf_op jit(solution)/shard_map/all_to_all | solution.py:31
  116.1 0.0 copy-start.2
  116.1 1.5 copy.7
  117.6 0.0 reduce-scatter.2.cloned.1.call-update
  117.6 40.3 %reduce-scatter.2.cloned.1.call-done = f32[1024,64]{0,1:T(8,128)} async-done(((f32[8192,64]{0,1:T(8,128)}), f32[1024,64]{0,1:T(8,128)}) %reduce-scatter.2.cloned.1.call-update) | async-done | bytes 262160 | tf_op jit(solution)/shard_map/reduce_scatter | solution.py:33
  158.0 0.0 copy-done.2
  158.0 0.0 copy-start.3
  158.0 3.7 %fusion.6 = f32[2048,64]{0,1:T(8,128)S(1)} fusion(bf16[2048,1024]{1,0:T(8,128)(2,1)} %param.8, pred[]{:T(512)S(6)} %eq.27, f32[1024,64]{0,1:T(8,128)} %reduce-scatter.2.cloned.1.call-done, bf16[1024,64]{0,1:T(8,128)(2,1)S(1)} %copy-done.2), kind=kOutput, calls=%fused_computation.10 | convolution fusion | flops 268763136 | bytes 5111809 | tf_op jit(solution)/shard_map/dot_general | solution.py:38
  161.7 29.6 %all-reduce.4 = bf16[2048,64]{0,1:T(8,128)(2,1)S(1)} all-reduce(f32[2048,64]{0,1:T(8,128)S(1)} %fusion.6), channel_id=1, replica_groups=mesh['blk'=8,'slab'=4] {'blk'}, use_global_device_ids=true, to_apply=%region_1.2 | all-reduce | flops 131072 | bytes 786432 | tf_op jit(solution)/shard_map/psum | solution.py:40
  191.3 0.0 copy-done.3
  191.3 0.0 copy-start
  191.3 3.7 %fusion.23 = f32[1024,64]{0,1:T(8,128)S(1)} fusion(f32[1024,64]{0,1:T(8,128)S(1)} %copy-done.3, bf16[2048,64]{0,1:T(8,128)(2,1)S(1)} %all-reduce.4, bf16[1024,8192]{1,0:T(8,128)(2,1)} %param.7, pred[]{:T(512)S(6)} %gt.9), kind=kOutput, calls=%fused_computation.24 | convolution fusion | flops 268566528 | bytes 4980737 | tf_op jit(solution)/shard_map/dot_general | solution.py:45
  195.1 0.0 copy-done
  195.1 1.4 fusion.7
  196.5 29.2 %all-reduce.5 = bf16[2048,64]{0,1:T(8,128)(2,1)S(1)} all-reduce(f32[2048,64]{0,1:T(8,128)S(1)} %fusion.7), channel_id=1, replica_groups=mesh['blk'=8,'slab'=4] {'blk'}, use_global_device_ids=true, to_apply=%region_2.3 | all-reduce | flops 131072 | bytes 786432 | tf_op jit(solution)/shard_map/psum | solution.py:40
  225.7 0.0 copy-start.1
  225.7 3.7 %fusion.32 = f32[1024,64]{0,1:T(8,128)S(1)} fusion(f32[1024,64]{0,1:T(8,128)S(1)} %fusion.23, bf16[2048,64]{0,1:T(8,128)(2,1)S(1)} %all-reduce.5, bf16[1024,8192]{1,0:T(8,128)(2,1)} %param.7, pred[]{:T(512)S(6)} %gt.10), kind=kOutput, calls=%fused_computation.27 | convolution fusion | flops 268566528 | bytes 4980737 | tf_op jit(solution)/shard_map/dot_general | solution.py:45
  229.4 0.0 copy-done.1
  229.4 1.4 fusion.8
  230.8 28.8 %all-reduce.6 = bf16[2048,64]{0,1:T(8,128)(2,1)S(1)} all-reduce(f32[2048,64]{0,1:T(8,128)S(1)} %fusion.8), channel_id=1, replica_groups=mesh['blk'=8,'slab'=4] {'blk'}, use_global_device_ids=true, to_apply=%region_3.4 | all-reduce | flops 131072 | bytes 786432 | tf_op jit(solution)/shard_map/psum | solution.py:40
  259.6 6.2 %fusion.9 = f32[2048,64]{0,1:T(8,128)S(1)} fusion(bf16[2048,1024]{1,0:T(8,128)(2,1)} %param.8, f32[1024,64]{0,1:T(8,128)S(1)} %fusion.32, bf16[2048,64]{0,1:T(8,128)(2,1)S(1)} %all-reduce.6, bf16[1024,8192]{1,0:T(8,128)(2,1)} %param.7, bf16[1024,64]{0,1:T(8,128)(2,1)S(1)} %copy-done.2, pred[]{:T(512)S(6)} %eq.24, pred[]{:T(512)S(6)} %gt.11), kind=kOutput, calls=%fused_computation.13 | convolution fusion | flops 537329664 | bytes 9568258 | tf_op jit(solution)/shard_map/dot_general | solution.py:38
  265.8 28.8 %all-reduce.7 = bf16[2048,64]{0,1:T(8,128)(2,1)S(1)} all-reduce(f32[2048,64]{0,1:T(8,128)S(1)} %fusion.9), channel_id=1, replica_groups=mesh['blk'=8,'slab'=4] {'blk'}, use_global_device_ids=true, to_apply=%region_4.5 | all-reduce | flops 131072 | bytes 786432 | tf_op jit(solution)/shard_map/psum | solution.py:40
  294.5 0.7 fusion.56
Async XLA Ops:
  6.5 151.4 %reduce-scatter.2.cloned.1.call-start = ((), (), s32[]{:S(2)}) async-start(), calls=%async_computation.2 | async-start | bytes 2359296 | tf_op jit(solution)/shard_map/reduce_scatter | solution.py:33
  6.5 12.4 %collective-permute-start = (bf16[3072,64]{0,1:T(8,128)(2,1)}, bf16[3072,64]{0,1:T(8,128)(2,1)S(1)}, u32[]{:S(2)}, u32[]{:S(2)}) collective-permute-start(bf16[3072,64]{0,1:T(8,128)(2,1)} %param.6), channel_id=1, source_target_pairs={{0,1},{1,0},{2,3},{3,2},{4,5},{5,4},{6,7},{7,6},{8,9},{9,8},{10,11... | collective-permute-start | bytes 1179656 | tf_op jit(solution)/shard_map/ppermute | solution.py:13
  20.3 36.5 %collective-permute-start.1 = (bf16[3072,128]{0,1:T(8,128)(2,1)S(1)}, bf16[3072,128]{0,1:T(8,128)(2,1)S(1)}, u32[]{:S(2)}, u32[]{:S(2)}) collective-permute-start(bf16[3072,128]{0,1:T(8,128)(2,1)S(1)} %maximum_select_fusion.2), channel_id=1, source_target_pairs={{0,2},{1,3},{2,0},{3,1},{4,6},{5,7},{6,4},{7,5},{8,10},{9,11},{10,... | collective-permute-start | bytes 2359304 | tf_op jit(solution)/shard_map/ppermute | solution.py:13
  116.1 41.9 %copy-start.2 = (bf16[1024,64]{0,1:T(8,128)(2,1)S(1)}, bf16[1024,64]{0,1:T(8,128)(2,1)}, u32[]{:S(2)}) copy-start(bf16[1024,64]{0,1:T(8,128)(2,1)} %param.9) | copy-start | bytes 393220
  158.0 33.4 %copy-start.3 = (f32[1024,64]{0,1:T(8,128)S(1)}, f32[1024,64]{0,1:T(8,128)}, u32[]{:S(2)}) copy-start(f32[1024,64]{0,1:T(8,128)} %reduce-scatter.2.cloned.1.call-done) | copy-start | bytes 786436
  191.3 3.7 %copy-start = (bf16[2048,1024]{1,0:T(8,128)(2,1)S(1)}, bf16[2048,1024]{1,0:T(8,128)(2,1)}, u32[]{:S(2)}) copy-start(bf16[2048,1024]{1,0:T(8,128)(2,1)} %param.8) | copy-start | bytes 12582916
  225.7 3.8 %copy-start.1 = (bf16[2048,1024]{1,0:T(8,128)(2,1)S(1)}, bf16[2048,1024]{1,0:T(8,128)(2,1)}, u32[]{:S(2)}) copy-start(bf16[2048,1024]{1,0:T(8,128)(2,1)} %param.8) | copy-start | bytes 12582916
Sparse Core Ops, SparseCore 0:
  117.7 40.1 reduce-scatter.1
